TPU v7x, 32 devices: a whole 2x2x4 slice. The times are simulated.
32 devices in a mesh: grp: 2 (over x), row: 16 (over z, y, core).
Axes of the slice: x: 2, y: 2, z: 4, core: 2. Of those that a mesh axis runs over, the one named last changes fastest.
Arguments:
- geometry: float32 [9, 16384], P(None, ('grp', 'row')), parts along dimension 1, as said below
- emission: float32 [16, 16384], P(None, ('grp', 'row')), parts along dimension 1, may hold values from 0.1 to 10
- reflect: float32 [16384], P(('grp', 'row')), parts along dimension 0, may hold values from 0.2 to 0.8
- occlusion: int32 [1024, 256], P(('grp', 'row')), parts along dimension 0, may hold values from 0 to 65535
- pair_recv: int32 [1024], P(('grp', 'row')), parts along dimension 0, may hold values from 0 to 31, as said below
- pair_src: int32 [1024], P(('grp', 'row')), parts along dimension 0, may hold values from 0 to 1
- pair_count: int32 [32], P(('grp', 'row')), parts along dimension 0, may hold values from 8 to 32, as said below
Outputs:
- radiosity: float32 [16, 16384], P(None, ('grp', 'row')), parts along dimension 1
- row_sums: float32 [16384], P(('grp', 'row')), parts along dimension 0
There are 2 independent parts, one for each index of `grp`. A program takes and returns all parts, laid end to end along the dimension named above; each array names one. Nothing has to cross between parts.
Inputs may be any that keep to these rules, and one draw needn't show every extreme that they name: `pair_recv`: in each index of row the 32 slots name distinct receiving tiles. `pair_count`: some index of row has all 32 slots live in every draw. `geometry`: edges are never parallel; every area is 0.2 or more.
All inputs are finite; a program needn't handle non-finite values.
Results may differ from a plain program's by a relative error of at most 0.0003.
Values sent between devices are 32-bit elements; how exact they have to be, the bound alone decides.
No kernel may reach another device: no remote copies, remote signals or barrier semaphores. Data moves between devices by JAX's collectives and lax.ppermute only.
A program may use at most 64 MiB of HBM per device.

v0:
```python
import functools
import math

import jax
import jax.numpy as jnp
from jax import lax
from jax.experimental import pallas as pl
from jax.experimental.pallas import tpu as pltpu
from jax.sharding import PartitionSpec as P

TILE = 256
GROUPS = 16
HOURS = 16
CH = 32
N_CH = TILE // CH
SPLIT_K = 48
BF16 = jnp.bfloat16
F32 = jnp.float32

LANES = 128
SHARED = 10
AREA_MIN = 0.2
NEAR = 4e-4


def to_bf16(x):
    return x.astype(BF16).astype(F32)


def split3(x, narrow=to_bf16):
    hi = narrow(x)
    rest = x - hi
    mid = narrow(rest)
    return hi, mid, rest - mid


def split2(x):
    hi = x.astype(BF16)
    return hi, (x - hi.astype(F32)).astype(BF16)


def cross_of(u, v):
    return (
        u[1] * v[2] - u[2] * v[1],
        u[2] * v[0] - u[0] * v[2],
        u[0] * v[1] - u[1] * v[0],
    )


def dot3(a, b):
    return a[0] * b[0] + a[1] * b[1] + a[2] * b[2]


def frame(geo, origin):
    corner = [geo[c] - origin[c] for c in range(3)]
    u = [geo[3 + c] for c in range(3)]
    v = [geo[6 + c] for c in range(3)]
    centre = [corner[c] + 0.5 * (u[c] + v[c]) for c in range(3)]
    e1 = [0.25 * (u[c] + v[c]) for c in range(3)]
    e2 = [0.25 * (u[c] - v[c]) for c in range(3)]
    cross = cross_of(u, v)
    area = jnp.sqrt(dot3(cross, cross))
    normal = [cross[c] / area for c in range(3)]
    offsets = [e1, [-x for x in e1], e2, [-x for x in e2]]
    return centre, offsets, normal, area


def across(row):
    parts = [
        jnp.transpose(jnp.broadcast_to(row[:, c : c + 128], (128, 128)))
        for c in range(0, row.shape[1], 128)
    ]
    return jnp.concatenate(parts, 0)


def recv_kernel(geo_ref, refl, left0, left1, left2, centres, refl_out, middle_out):
    geo = [geo_ref[c : c + 1] for c in range(9)]
    origin = [jnp.mean(geo[c], 1, keepdims=True) for c in range(3)]
    middle_out[...] = jnp.concatenate(
        [jnp.broadcast_to(x, (1, LANES)) for x in origin] + [jnp.zeros((5, LANES), F32)], 0
    )
    centre, offsets, normal, _ = frame(geo, origin)
    one = jnp.ones_like(centre[0])
    zero = jnp.zeros_like(one)

    def columns(rows):
        hi, mid, lo = split3(jnp.concatenate(rows, 0))
        pad = [jnp.zeros_like(hi)] * ((128 - SPLIT_K) // 8)
        wide = jnp.concatenate([hi, hi, hi, mid, mid, lo] + pad, 0)
        return jnp.transpose(wide)[:, :SPLIT_K].astype(BF16)

    for p, a in enumerate(offsets):
        point = [centre[c] + a[c] for c in range(3)]
        cols0 = columns(point + [dot3(point, point), one] + [zero] * 3)
        cols1 = columns(point + list(a) + [one, dot3(a, a) + 2.0 * dot3(centre, a)])
        for c in range(left1.shape[0]):
            rows = slice(c * CH, (c + 1) * CH)
            left0[c, p * CH : (p + 1) * CH, :] = cols0[rows]
            left1[c, p * CH : (p + 1) * CH, :] = cols1[rows]
    left2[...] = columns(list(normal) + [-dot3(normal, centre)] + [zero] * 4)
    for c in range(3):
        centres[c] = across(centre[c])
    refl_out[...] = refl[...]


def recv_factors(geometry, reflect):
    width = geometry.shape[1]
    vmem = pl.BlockSpec(memory_space=pltpu.VMEM)
    return pl.pallas_call(
        recv_kernel,
        out_shape=(
            jax.ShapeDtypeStruct((width // CH, 4 * CH, SPLIT_K), BF16),
            jax.ShapeDtypeStruct((width // CH, 4 * CH, SPLIT_K), BF16),
            jax.ShapeDtypeStruct((width, SPLIT_K), BF16),
            jax.ShapeDtypeStruct((3, width, 128), F32),
            jax.ShapeDtypeStruct((1, width), F32),
            jax.ShapeDtypeStruct((8, LANES), F32),
        ),
        in_specs=[vmem] * 2,
        out_specs=(vmem,) * 6,
        cost_estimate=pl.CostEstimate(flops=200000, bytes_accessed=1600000, transcendentals=1024),
        compiler_params=pltpu.CompilerParams(vmem_limit_bytes=4 << 20),
        name="recv_factors",
    )(geometry, reflect)


def pack_kernel(
    count, recv_h, src_h, geo_h, emis_h, occ_h, shared, words,
    recv, src, geo, emis, occ, sem,
):
    chunks = emis.shape[1] // LANES
    own = emis.shape[1] // TILE
    me = lax.axis_index("row")
    copies = [
        pltpu.make_async_copy(a, b, sem.at[i])
        for i, (a, b) in enumerate(
            ((recv_h, recv), (src_h, src), (geo_h, geo), (emis_h, emis), (occ_h, occ))
        )
    ]
    for copy in copies:
        copy.start()
    words[...] = jnp.zeros_like(words)
    for copy in copies:
        copy.wait()
    for c in range(chunks):
        lanes = slice(c * LANES, (c + 1) * LANES)
        shared[c * HOURS : (c + 1) * HOURS, :] = emis[:, lanes]
        start = chunks * HOURS + c * SHARED
        shared[start : start + 9, :] = geo[:, lanes]
        shared[start + 9 : start + 10, :] = jnp.zeros((1, LANES), F32)
    lane = lax.broadcasted_iota(jnp.int32, (1, LANES), 1)

    def slot(k, code):
        tile = recv[k]
        owner = tile // own
        row = 2 * (tile - owner * own)
        line = occ[pl.ds(k, 1), :].astype(F32)
        for c in range(2):
            words[owner ^ me, pl.ds(row + c, 1), :] = line[:, c * LANES : (c + 1) * LANES]
        return jnp.where(lane == tile, 1 + src[k], code)

    code = lax.fori_loop(0, count[0], slot, jnp.zeros_like(lane))
    start = chunks * HOURS + 9
    shared[start : start + 1, :] = code.astype(F32)


def pack(geometry, emission, occlusion, pair_recv, pair_src, pair_count):
    vmem = pl.BlockSpec(memory_space=pltpu.VMEM)
    smem = pl.BlockSpec(memory_space=pltpu.SMEM)
    hbm = pl.BlockSpec(memory_space=pltpu.HBM)
    width = geometry.shape[1]
    n_dev = lax.axis_size("row")
    large = [
        pltpu.with_memory_space_constraint(x, pltpu.HBM)
        for x in (pair_recv, pair_src, geometry, emission, occlusion)
    ]
    return pl.pallas_call(
        pack_kernel,
        out_shape=(
            jax.ShapeDtypeStruct((width // LANES * (HOURS + SHARED), LANES), F32),
            jax.ShapeDtypeStruct((n_dev, width // LANES, LANES), F32),
        ),
        in_specs=[smem] + [hbm] * 5,
        out_specs=(vmem, vmem),
        scratch_shapes=[
            pltpu.SMEM(pair_recv.shape, jnp.int32),
            pltpu.SMEM(pair_src.shape, jnp.int32),
            pltpu.VMEM(geometry.shape, F32),
            pltpu.VMEM(emission.shape, F32),
            pltpu.VMEM(occlusion.shape, jnp.int32),
            pltpu.SemaphoreType.DMA((5,)),
        ],
        compiler_params=pltpu.CompilerParams(vmem_limit_bytes=4 << 20),
        name="pack",
    )(pair_count, *large)


def source_factors(geo, origin, exact, rhs1, rhs2, middle):
    centre, offsets, normal, area = frame(geo, origin)
    one = jnp.ones_like(area)
    zero = jnp.zeros_like(area)

    def put(ref, col, rows):
        hi, mid, lo = split3(jnp.concatenate(rows, 0))
        ref[:, col * TILE : (col + 1) * TILE] = jnp.concatenate(
            [hi, mid, lo, hi, mid, hi], 0
        ).astype(BF16)

    if exact:
        m2 = [-2.0 * x for x in centre]
        for q, b in enumerate(offsets):
            rest = dot3(b, b) + 2.0 * dot3(centre, b) + 0.25 * area
            put(rhs1, q, [-2.0 * x for x in b] + m2 + [rest, one])
        put(rhs1, 4, list(normal) + [zero] * 3 + [-dot3(normal, centre), zero])
    else:
        for q, b in enumerate(offsets):
            point = [centre[c] + b[c] for c in range(3)]
            rest = dot3(point, point) + 0.25 * area
            put(rhs1, q, [-2.0 * x for x in point] + [one, rest] + [zero] * 3)
        put(rhs1, 4, list(normal) + [zero, -dot3(normal, centre)] + [zero] * 3)
    weight = area * (1.0 / (16.0 * math.pi))
    for q, b in enumerate(offsets):
        put(
            rhs2,
            q,
            [(centre[c] + b[c]) * weight for c in range(3)] + [weight] + [zero] * 4,
        )
    if exact:
        for c in range(3):
            middle[c : c + 1, :] = centre[c]


def mm(a, b):
    return lax.dot_general(a, b, (((1,), (0,)), ((), ())), preferred_element_type=F32)


def mm_t(a, b):
    return lax.dot_general(a, b, (((1,), (1,)), ((), ())), preferred_element_type=F32)


def inverse_square(t):
    return 1.0 / (t * t)


def block_kernel(
    begin, last, pay, words, left0, left1, left2, centres, refl, origin_ref, *refs
):
    if last:
        so_far_hi, so_far_lo, blocks, order, out_b, out_sums, out_scale, *refs = refs
        acc_hi, acc_lo, *refs = refs
    else:
        blocks, order, acc_hi, acc_lo, *refs = refs
    (
        rhs1, rhs2, middle, next1, next2, next_middle, word_s, code_v, code, code_sem,
    ) = refs
    n_dev = pay.shape[0]
    own = refl.shape[1] // TILE
    pairs = own * n_dev
    chunks = refl.shape[1] // LANES
    geo_row = chunks * HOURS
    origin = [origin_ref[c : c + 1, 0:1] for c in range(3)]
    lane = lax.broadcasted_iota(jnp.int32, (1, LANES), 1)
    first = own * lax.axis_index("row")
    wide = lax.broadcasted_iota(jnp.int32, (n_dev, LANES), 1)
    table = jnp.zeros((n_dev, LANES), F32)
    rows = pay[:, geo_row + 9, :]
    for r in range(own):
        here = jnp.sum(jnp.where(lane == first + r, rows, 0.0), 1, keepdims=True)
        table = jnp.where(wide == r, here, table)
    far = [jnp.zeros((n_dev, LANES), F32)] * 3
    for c in range(chunks):
        for part in range(3):
            at = geo_row + SHARED * c + 3 * part
            v = [pay[:, at + x, :] for x in range(3)]
            if part == 0:
                v = [v[x] - origin[x] for x in range(3)]
            far[part] = jnp.maximum(far[part], dot3(v, v))
    reach = sum(jnp.sqrt(jnp.max(f)) for f in far)
    near = 2.0 * reach * reach * 2.0**-23 <= NEAR * 0.25 * AREA_MIN
    code_v[...] = table.astype(jnp.int32)
    to_scalar = pltpu.make_async_copy(code_v, code, code_sem)
    to_scalar.start()
    acc_hi[...] = so_far_hi[...] if last else jnp.zeros_like(acc_hi)
    acc_lo[...] = so_far_lo[...] if last else jnp.zeros_like(acc_lo)
    lane = lax.broadcasted_iota(jnp.int32, (1, TILE), 1)
    group_bit = jnp.left_shift(1, lane // (TILE // GROUPS))
    to_scalar.wait()

    order[0] = 0

    n = jnp.int32(0)
    for r in range(own):

        def listed(j, count):
            value = code[j, r]
            order[1 + count] = jnp.maximum(value - 1, 0) * pairs + r * n_dev + j
            return count + (value > 0).astype(jnp.int32)

        n = lax.fori_loop(begin, n_dev, listed, n, unroll=4)
    order[0] = n
    order[1 + n] = 0

    def where_is(i):
        entry = order[1 + i]
        value = entry // pairs
        k = entry - value * pairs
        r = k // n_dev
        return r, k - r * n_dev, value

    def prepare(i, exact):
        _, j, source = where_is(i)
        at = geo_row + 2 * SHARED * source
        geo = [
            jnp.concatenate(
                [pay[j, pl.ds(at + c, 1), :], pay[j, pl.ds(at + SHARED + c, 1), :]], 1
            )
            for c in range(9)
        ]
        source_factors(geo, origin, exact, next1, next2, next_middle)

    def deposit(i):
        r, j, source = where_is(i)
        at = pl.multiple_of(2 * HOURS * source, HOURS)
        x = jnp.concatenate(
            [pay[j, pl.ds(at, HOURS), :], pay[j, pl.ds(at + HOURS, HOURS), :]], 1
        )
        x_hi, x_lo = split2(x)
        ones = jnp.ones((16, TILE), BF16)
        acc_hi[r] += mm_t(jnp.concatenate([x_hi, x_lo, ones], 0), blocks[i, 0])
        acc_lo[r] += mm_t(jnp.concatenate([x_hi, ones], 0), blocks[i, 1])

    def pair(exact, i, carry):
        r, j, _ = where_is(i)
        rhs1[...] = next1[...]
        rhs2[...] = next2[...]
        if exact:
            middle[...] = next_middle[...]
        for c in range(2):
            word_s[c * LANES : (c + 1) * LANES, :] = across(
                words[j, pl.ds(2 * r + c, 1), :].astype(jnp.int32)
            )
        prepare(i + 1, exact)
        for c in range(N_CH):
            rows = slice(c * CH, (c + 1) * CH)
            own_rows = pl.ds(pl.multiple_of(r * TILE + c * CH, CH), CH)
            lhs2 = left2[own_rows, :]
            lhs1 = (left1 if exact else left0)[r * N_CH + c]
            s = None
            for x in range(3 if exact else 0):
                mine = centres[x, own_rows, :]
                d = middle[x : x + 1, :] - jnp.concatenate([mine, mine], 1)
                s = d * d if s is None else s + d * d
            facing = jnp.maximum(mm(lhs1, rhs1[:, 4 * TILE : 5 * TILE]), 0.0)
            total = None
            for q in range(4):
                cols = slice(q * TILE, (q + 1) * TILE)
                rest = mm(lhs1, rhs1[:, cols])
                part = None
                for p in range(4):
                    pr = slice(p * CH, (p + 1) * CH)
                    t = s + rest[pr] if exact else rest[pr]
                    term = facing[pr] * inverse_square(t)
                    part = term if part is None else part + term
                a = jnp.maximum(mm(lhs2, rhs2[:, cols]), 0.0) * part
                total = a if total is None else total + a
            w = word_s[rows, :]
            w = jnp.concatenate([w, w], 1)
            total = jnp.where((w & group_bit) != 0, total, 0.0)
            hi, lo = split2(total)
            blocks[i, 0, rows, :] = hi
            blocks[i, 1, rows, :] = lo
        deposit(i)
        return carry

    for exact in (False, True):

        @pl.when(jnp.logical_not(near) if exact else near)
        def _():
            prepare(0, exact)
            lax.fori_loop(0, n, functools.partial(pair, exact), 0)

    if not last:
        return
    for r in range(own):
        cols = slice(r * TILE, (r + 1) * TILE)
        irr = acc_hi[r, 0:16] + acc_hi[r, 16:32] + acc_lo[r, 0:16]
        sums = acc_hi[r, 32:33] + acc_lo[r, 16:17]
        scale = refl[:, cols] / jnp.maximum(sums, 1.0)
        out_sums[:, cols] = sums
        out_scale[:, cols] = scale
        emis = [pay[0, c * HOURS : (c + 1) * HOURS, :] for c in (2 * r, 2 * r + 1)]
        out_b[:, cols] = jnp.concatenate(emis, 1) + scale * irr


def view_blocks(begin, pay, words, left, so_far=None):
    vmem = pl.BlockSpec(memory_space=pltpu.VMEM)
    n_dev = pay.shape[0]
    width = left[4].shape[1]
    own = width // TILE
    pairs = own * n_dev
    sums = [
        jax.ShapeDtypeStruct((own, 48, TILE), F32),
        jax.ShapeDtypeStruct((own, 32, TILE), F32),
    ]
    outs = [
        jax.ShapeDtypeStruct((own * (n_dev - begin), 2, TILE, TILE), BF16),
        jax.ShapeDtypeStruct((2 * pairs,), jnp.int32),
    ]
    scratch = []
    if so_far is None:
        outs += sums
    else:
        outs += [jax.ShapeDtypeStruct((x, width), F32) for x in (HOURS, 1, 1)]
        scratch += [pltpu.VMEM(x.shape, F32) for x in sums]
    args = [pay, words, *left, *(so_far or ())]
    work = own * (n_dev - begin) // 2
    return pl.pallas_call(
        functools.partial(block_kernel, begin, so_far is not None),
        out_shape=outs,
        in_specs=[vmem] * len(args),
        out_specs=[vmem, pl.BlockSpec(memory_space=pltpu.SMEM)] + [vmem] * (len(outs) - 2),
        scratch_shapes=scratch
        + [
            pltpu.VMEM((SPLIT_K, 5 * TILE), BF16),
            pltpu.VMEM((SPLIT_K, 4 * TILE), BF16),
            pltpu.VMEM((8, TILE), F32),
            pltpu.VMEM((SPLIT_K, 5 * TILE), BF16),
            pltpu.VMEM((SPLIT_K, 4 * TILE), BF16),
            pltpu.VMEM((8, TILE), F32),
            pltpu.VMEM((TILE, 128), jnp.int32),
            pltpu.VMEM((n_dev, 128), jnp.int32),
            pltpu.SMEM((n_dev, 128), jnp.int32),
            pltpu.SemaphoreType.DMA,
        ],
        compiler_params=pltpu.CompilerParams(vmem_limit_bytes=12 << 20),
        cost_estimate=pl.CostEstimate(
            flops=work * 10**9, bytes_accessed=work << 18, transcendentals=work << 20
        ),
        name="view_blocks",
    )(*args)


def bounce_kernel(order0, order1, field, blocks0, blocks1, scale, emis, out, acc):
    own = out.shape[1] // TILE
    acc[...] = jnp.zeros_like(acc)

    def some(order, blocks, step, carry):
        pairs = order.shape[0] // 2
        n_dev = pairs // own
        for b in range(4):
            i = 4 * step + b
            live = i < order[0]
            entry = jnp.where(live, order[jnp.minimum(1 + i, 2 * pairs - 1)], 0)
            source = entry // pairs
            k = entry - source * pairs
            r = k // n_dev
            j = k - r * n_dev
            at = jnp.minimum(i, blocks.shape[0] - 1)
            lanes = pl.ds(pl.multiple_of(source * TILE, TILE), TILE)
            x_hi, x_lo = split2(field[j, :, lanes])
            both = mm_t(jnp.concatenate([x_hi, x_lo], 0), blocks[at, 0])
            got = both[0:16] + both[16:32] + mm_t(x_hi, blocks[at, 1])
            acc[r] += jnp.where(live, got, 0.0)
        return carry

    for order, blocks in ((order0, blocks0), (order1, blocks1)):
        lax.fori_loop(0, (order[0] + 3) // 4, functools.partial(some, order, blocks), 0)
    for r in range(own):
        cols = slice(r * TILE, (r + 1) * TILE)
        out[:, cols] = emis[:, cols] + scale[:, cols] * acc[r]


def second_bounce(orders, field, blocks, scale, emission):
    vmem = pl.BlockSpec(memory_space=pltpu.VMEM)
    own = emission.shape[1] // TILE
    return pl.pallas_call(
        bounce_kernel,
        out_shape=jax.ShapeDtypeStruct(emission.shape, F32),
        in_specs=[pl.BlockSpec(memory_space=pltpu.SMEM)] * 2 + [vmem] * 5,
        out_specs=vmem,
        scratch_shapes=[pltpu.VMEM((own, HOURS, TILE), F32)],
        compiler_params=pltpu.CompilerParams(vmem_limit_bytes=12 << 20),
        name="second_bounce",
    )(*orders, field, *blocks, scale, emission)


def gather_rounds(x, n_dev):
    held = x[None]
    step = n_dev // 2
    while step:
        other = lax.ppermute(held, "row", [(i, i ^ step) for i in range(n_dev)])
        held = jnp.concatenate([held, other], 0)
        step //= 2
    return held


def on_device(geometry, emission, reflect, occlusion, pair_recv, pair_src, pair_count):
    n_dev = lax.axis_size("row")
    shared, words = pack(geometry, emission, occlusion, pair_recv, pair_src, pair_count)
    left = recv_factors(geometry, reflect[None])
    held, words = shared[None], words[None]
    step = n_dev // 2
    while step:
        lines = held.shape[0] * held.shape[1]
        keep, send = words[:, :step], words[:, step:]
        message = jnp.concatenate([held.reshape(-1, LANES), send.reshape(-1, LANES)], 0)
        other = lax.ppermute(message, "row", [(i, i ^ step) for i in range(n_dev)])
        if step == n_dev // 4:
            other, left = lax.optimization_barrier((other, left))
        if step == 2:
            begin = held.shape[0]
            early = view_blocks(0, held, words[:, 0], left)
            other, early = lax.optimization_barrier((other, early))
        held = jnp.concatenate([held, other[:lines].reshape(held.shape)], 0)
        words = jnp.concatenate([keep, other[lines:].reshape(send.shape)], 0)
        step //= 2
    blocks0, order0, *so_far = early
    blocks1, order1, field, sums, scale = view_blocks(
        begin, held, words[:, 0], left, so_far
    )
    fields = gather_rounds(field, n_dev)
    radiosity = second_bounce(
        (order0, order1), fields, (blocks0, blocks1), scale, emission
    )
    return (radiosity, sums[0])


def solution(mesh):
    placed = (
        P(None, ("grp", "row")),
        P(None, ("grp", "row")),
        P(("grp", "row")),
        P(("grp", "row"), None),
        P(("grp", "row")),
        P(("grp", "row")),
        P(("grp", "row")),
    )
    return jax.shard_map(
        on_device,
        mesh=mesh,
        in_specs=placed,
        out_specs=(P(None, ("grp", "row")), P(("grp", "row"))),
        check_vma=False,
    )
```

profile of v0, /device:TPU:1, one launch (start us, length us, event | category | flops | bytes accessed | tf_op | source)
XLA Modules:
  0.0 59.5 jit_solution(15672850960283971652)
XLA Ops:
  1.3 1.0 %pack.1 = (f32[104,128]{1,0:T(8,128)S(1)}, f32[16,4,128]{2,1,0:T(4,128)S(1)}) custom-call(s32[1]{0:T(128)S(6)} %copy.29.count, s32[32]{0:T(128)} %recv_h.1, s32[32]{0:T(128)} %src_h.1, f32[9,512]{1,0:T(8,128)} %geo_ref.1, f32[16,512]{1,0:T(8,128)} %emis.1, s32[32,256]{1,0:T(8,128)} %occ_h.1), custom_call_target="tpu_custom_call" | custom-call | tf_op jit(solution)/shard_map/pack/pallas_call | solution.py:177
  2.3 3.2 %collective-permute-start = (f32[136,128]{1,0:T(8,128)S(1)}, f32[136,128]{1,0:T(8,128)S(1)}, u32[]{:S(2)}, u32[]{:S(2)}) collective-permute-start(f32[136,128]{1,0:T(8,128)S(1)} %pad_maximum_fusion.8), channel_id=1, source_target_pairs={{0,8},{1,9},{2,10},{3,11},{4,12},{5,13},{6,14},{7,15},{8,0},{9,1},... | collective-permute-start | bytes 208904 | tf_op jit(solution)/shard_map/ppermute | solution.py:507
  5.5 0.0 copy-start.1
  5.5 0.8 %copy-done.1 = f32[9,512]{1,0:T(8,128)S(1)} copy-done((f32[9,512]{1,0:T(8,128)S(1)}, f32[9,512]{1,0:T(8,128)}, u32[]{:S(2)}) %copy-start.1) | copy-done | bytes 18456
  6.2 0.0 copy-start.2
  6.2 0.7 %copy-done.2 = f32[512]{0:T(512)S(1)} copy-done((f32[512]{0:T(512)S(1)}, f32[512]{0:T(512)}, u32[]{:S(2)}) %copy-start.2) | copy-done | bytes 2072
  6.9 0.7 %recv_factors.1 = (bf16[16,128,48]{2,1,0:T(8,128)(2,1)S(1)}, bf16[16,128,48]{2,1,0:T(8,128)(2,1)S(1)}, bf16[512,48]{1,0:T(8,128)(2,1)S(1)}, f32[3,512,128]{2,1,0...) custom-call(f32[9,512]{1,0:T(8,128)S(1)} %copy-done.1, f32[1,512]{1,0:T(1,128)S(1)} %bitcast.38), custom_call_target="tpu_custom_call" | custom-call | flops 200000 | bytes 1600000 | tf_op jit(solution)/shard_map/recv_factors/pallas_call | solution.py:109
  7.6 0.0 collective-permute-done
  7.7 2.0 %collective-permute-start.1 = (f32[240,128]{1,0:T(8,128)S(1)}, f32[240,128]{1,0:T(8,128)S(1)}, u32[]{:S(2)}, u32[]{:S(2)}) collective-permute-start(f32[240,128]{1,0:T(8,128)S(1)} %pad_maximum_fusion.6), channel_id=1, source_target_pairs={{0,4},{1,5},{2,6},{3,7},{4,0},{5,1},{6,2},{7,3},{8,12},{9,13},{10,... | collective-permute-start | bytes 368648 | tf_op jit(solution)/shard_map/ppermute | solution.py:507
  9.6 2.3 %collective-permute-done.1 = f32[240,128]{1,0:T(8,128)S(1)} collective-permute-done((f32[240,128]{1,0:T(8,128)S(1)}, f32[240,128]{1,0:T(8,128)S(1)}, u32[]{:S(2)}, u32[]{:S(2)}) %collective-permute-start.1) | collective-permute-done | bytes 122912 | tf_op jit(solution)/shard_map/ppermute | solution.py:507
  12.0 1.5 %collective-permute-start.2 = (f32[448,128]{1,0:T(8,128)S(1)}, f32[448,128]{1,0:T(8,128)S(1)}, u32[]{:S(2)}, u32[]{:S(2)}) collective-permute-start(f32[448,128]{1,0:T(8,128)S(1)} %pad_maximum_fusion.3), channel_id=1, source_target_pairs={{0,2},{1,3},{2,0},{3,1},{4,6},{5,7},{6,4},{7,5},{8,10},{9,11},{10,... | collective-permute-start | bytes 688136 | tf_op jit(solution)/shard_map/ppermute | solution.py:507
  13.5 4.9 %view_blocks.2 = (bf16[8,2,256,256]{3,2,1,0:T(8,128)(2,1)S(1)}, s32[16]{0:T(128)S(1)}, f32[2,48,256]{2,1,0:T(8,128)S(1)}, f32[2,32,256]{2,1,0:T(8,128)S(1)}) custom-call(f32[4,104,128]{2,1,0:T(8,128)S(1)} %pad_maximum_fusion.4.pay, f32[4,4,128]{2,1,0:T(4,128)S(1)} %maximum_bitcast_fusion.words, bf16[16,128,48]{2,1,0:T(8,128)(2,1)S(1)} %get-tuple-element.40.left0, ...), custom_call_target="tpu_custom_call" | custom-call | flops 4000000000 | bytes 1048576 | tf_op jit(solution)/shard_map/view_blocks/pallas_call | solution.py:417
  18.4 0.0 collective-permute-done.2
  18.5 3.1 %collective-permute-start.3 = (f32[864,128]{1,0:T(8,128)S(1)}, f32[864,128]{1,0:T(8,128)S(1)}, u32[]{:S(2)}, u32[]{:S(2)}) collective-permute-start(f32[864,128]{1,0:T(8,128)S(1)} %pad_maximum_fusion), channel_id=1, source_target_pairs={{0,1},{1,0},{2,3},{3,2},{4,5},{5,4},{6,7},{7,6},{8,9},{9,8},{10,11... | collective-permute-start | bytes 1327112 | tf_op jit(solution)/shard_map/ppermute | solution.py:507
  21.7 1.4 %collective-permute-done.3 = f32[864,128]{1,0:T(8,128)S(1)} collective-permute-done((f32[864,128]{1,0:T(8,128)S(1)}, f32[864,128]{1,0:T(8,128)S(1)}, u32[]{:S(2)}, u32[]{:S(2)}) %collective-permute-start.3) | collective-permute-done | bytes 442400 | tf_op jit(solution)/shard_map/ppermute | solution.py:507
  23.2 0.0 copy-start
  23.2 13.2 %view_blocks.3 = (bf16[24,2,256,256]{3,2,1,0:T(8,128)(2,1)S(1)}, s32[64]{0:T(128)S(1)}, f32[16,512]{1,0:T(8,128)S(1)}, f32[1,512]{1,0:T(1,128)}, f32[1,512]{1,0:T(1,128)S(1)}) custom-call(f32[16,104,128]{2,1,0:T(8,128)S(1)} %constant_dynamic-update-slice_fusion.pay, f32[16,4,128]{2,1,0:T(4,128)S(1)} %fusion.1.words, ...), custom_call_target="tpu_custom_call" | custom-call | flops 12000000000 | bytes 3145728 | tf_op jit(solution)/shard_map/view_blocks/pallas_call | solution.py:417
  36.5 2.5 %collective-permute-start.4 = (f32[1,16,512]{2,1,0:T(8,128)S(1)}, f32[1,16,512]{2,1,0:T(8,128)S(1)}, u32[]{:S(2)}, u32[]{:S(2)}) collective-permute-start(f32[1,16,512]{2,1,0:T(8,128)S(1)} %bitcast.33), channel_id=1, source_target_pairs={{0,8},{1,9},{2,10},{3,11},{4,12},{5,13},{6,14},{7,15},{8,0},{9,1},... | collective-permute-start | bytes 98312 | tf_op jit(solution)/shard_map/ppermute | solution.py:491
  39.0 1.3 %collective-permute-done.4 = f32[1,16,512]{2,1,0:T(8,128)S(1)} collective-permute-done((f32[1,16,512]{2,1,0:T(8,128)S(1)}, f32[1,16,512]{2,1,0:T(8,128)S(1)}, u32[]{:S(2)}, u32[]{:S(2)}) %collective-permute-start.4) | collective-permute-done | bytes 32800 | tf_op jit(solution)/shard_map/ppermute | solution.py:491
  40.3 7.2 %collective-permute-start.5 = (f32[2,16,512]{2,1,0:T(8,128)S(1)}, f32[2,16,512]{2,1,0:T(8,128)S(1)}, u32[]{:S(2)}, u32[]{:S(2)}) collective-permute-start(f32[2,16,512]{2,1,0:T(8,128)S(1)} %pad_maximum_fusion.9), channel_id=1, source_target_pairs={{0,4},{1,5},{2,6},{3,7},{4,0},{5,1},{6,2},{7,3},{8,12},{9,13},{10,... | collective-permute-start | bytes 196616 | tf_op jit(solution)/shard_map/ppermute | solution.py:491
  47.4 2.0 %collective-permute-done.5 = f32[2,16,512]{2,1,0:T(8,128)S(1)} collective-permute-done((f32[2,16,512]{2,1,0:T(8,128)S(1)}, f32[2,16,512]{2,1,0:T(8,128)S(1)}, u32[]{:S(2)}, u32[]{:S(2)}) %collective-permute-start.5) | collective-permute-done | bytes 65568 | tf_op jit(solution)/shard_map/ppermute | solution.py:491
  49.4 0.1 collective-permute-start.6
  49.5 4.7 %collective-permute-done.6 = f32[4,16,512]{2,1,0:T(8,128)S(1)} collective-permute-done((f32[4,16,512]{2,1,0:T(8,128)S(1)}, f32[4,16,512]{2,1,0:T(8,128)S(1)}, u32[]{:S(2)}, u32[]{:S(2)}) %collective-permute-start.6) | collective-permute-done | bytes 131104 | tf_op jit(solution)/shard_map/ppermute | solution.py:491
  54.2 1.3 %collective-permute-start.7 = (f32[8,16,512]{2,1,0:T(8,128)S(1)}, f32[8,16,512]{2,1,0:T(8,128)S(1)}, u32[]{:S(2)}, u32[]{:S(2)}) collective-permute-start(f32[8,16,512]{2,1,0:T(8,128)S(1)} %pad_maximum_fusion.2), channel_id=1, source_target_pairs={{0,1},{1,0},{2,3},{3,2},{4,5},{5,4},{6,7},{7,6},{8,9},{9,8},{10,11... | collective-permute-start | bytes 786440 | tf_op jit(solution)/shard_map/ppermute | solution.py:491
  55.5 1.1 %collective-permute-done.7 = f32[8,16,512]{2,1,0:T(8,128)S(1)} collective-permute-done((f32[8,16,512]{2,1,0:T(8,128)S(1)}, f32[8,16,512]{2,1,0:T(8,128)S(1)}, u32[]{:S(2)}, u32[]{:S(2)}) %collective-permute-start.7) | collective-permute-done | bytes 262176 | tf_op jit(solution)/shard_map/ppermute | solution.py:491
  56.7 0.0 copy-done
  56.7 2.8 %second_bounce.1 = f32[16,512]{1,0:T(8,128)} custom-call(s32[16]{0:T(128)S(1)} %get-tuple-element.50.order0, s32[64]{0:T(128)S(1)} %get-tuple-element.54.order1, f32[16,16,512]{2,1,0:T(8,128)S(1)} %constant_dynamic-update-slice_fusion.5.field, bf16[8,2,256,256]{3,2,1,0:T(8,128)(2,1)S(1)} %get-tuple-element.56.blocks0, ...), custom_call_target="tpu_custom_call" | custom-call | tf_op jit(solution)/shard_map/second_bounce/pallas_call | solution.py:476
  (37 shorter events, 0.4 us)
Async XLA Ops:
  2.3 5.3 %collective-permute-start = (f32[136,128]{1,0:T(8,128)S(1)}, f32[136,128]{1,0:T(8,128)S(1)}, u32[]{:S(2)}, u32[]{:S(2)}) collective-permute-start(f32[136,128]{1,0:T(8,128)S(1)} %pad_maximum_fusion.8), channel_id=1, source_target_pairs={{0,8},{1,9},{2,10},{3,11},{4,12},{5,13},{6,14},{7,15},{8,0},{9,1},... | collective-permute-start | bytes 208904 | tf_op jit(solution)/shard_map/ppermute | solution.py:507
  5.5 0.8 %copy-start.1 = (f32[9,512]{1,0:T(8,128)S(1)}, f32[9,512]{1,0:T(8,128)}, u32[]{:S(2)}) copy-start(f32[9,512]{1,0:T(8,128)} %geo_ref.1) | copy-start | bytes 55300
  6.2 0.7 %copy-start.2 = (f32[512]{0:T(512)S(1)}, f32[512]{0:T(512)}, u32[]{:S(2)}) copy-start(f32[512]{0:T(512)} %param.9) | copy-start | bytes 6148
  7.7 4.2 %collective-permute-start.1 = (f32[240,128]{1,0:T(8,128)S(1)}, f32[240,128]{1,0:T(8,128)S(1)}, u32[]{:S(2)}, u32[]{:S(2)}) collective-permute-start(f32[240,128]{1,0:T(8,128)S(1)} %pad_maximum_fusion.6), channel_id=1, source_target_pairs={{0,4},{1,5},{2,6},{3,7},{4,0},{5,1},{6,2},{7,3},{8,12},{9,13},{10,... | collective-permute-start | bytes 368648 | tf_op jit(solution)/shard_map/ppermute | solution.py:507
  12.0 6.4 %collective-permute-start.2 = (f32[448,128]{1,0:T(8,128)S(1)}, f32[448,128]{1,0:T(8,128)S(1)}, u32[]{:S(2)}, u32[]{:S(2)}) collective-permute-start(f32[448,128]{1,0:T(8,128)S(1)} %pad_maximum_fusion.3), channel_id=1, source_target_pairs={{0,2},{1,3},{2,0},{3,1},{4,6},{5,7},{6,4},{7,5},{8,10},{9,11},{10,... | collective-permute-start | bytes 688136 | tf_op jit(solution)/shard_map/ppermute | solution.py:507
  18.5 4.6 %collective-permute-start.3 = (f32[864,128]{1,0:T(8,128)S(1)}, f32[864,128]{1,0:T(8,128)S(1)}, u32[]{:S(2)}, u32[]{:S(2)}) collective-permute-start(f32[864,128]{1,0:T(8,128)S(1)} %pad_maximum_fusion), channel_id=1, source_target_pairs={{0,1},{1,0},{2,3},{3,2},{4,5},{5,4},{6,7},{7,6},{8,9},{9,8},{10,11... | collective-permute-start | bytes 1327112 | tf_op jit(solution)/shard_map/ppermute | solution.py:507
  23.2 33.5 %copy-start = (f32[16,512]{1,0:T(8,128)S(1)}, f32[16,512]{1,0:T(8,128)}, u32[]{:S(2)}) copy-start(f32[16,512]{1,0:T(8,128)} %emis.1) | copy-start | bytes 98308
  36.5 3.8 %collective-permute-start.4 = (f32[1,16,512]{2,1,0:T(8,128)S(1)}, f32[1,16,512]{2,1,0:T(8,128)S(1)}, u32[]{:S(2)}, u32[]{:S(2)}) collective-permute-start(f32[1,16,512]{2,1,0:T(8,128)S(1)} %bitcast.33), channel_id=1, source_target_pairs={{0,8},{1,9},{2,10},{3,11},{4,12},{5,13},{6,14},{7,15},{8,0},{9,1},... | collective-permute-start | bytes 98312 | tf_op jit(solution)/shard_map/ppermute | solution.py:491
  40.3 9.1 %collective-permute-start.5 = (f32[2,16,512]{2,1,0:T(8,128)S(1)}, f32[2,16,512]{2,1,0:T(8,128)S(1)}, u32[]{:S(2)}, u32[]{:S(2)}) collective-permute-start(f32[2,16,512]{2,1,0:T(8,128)S(1)} %pad_maximum_fusion.9), channel_id=1, source_target_pairs={{0,4},{1,5},{2,6},{3,7},{4,0},{5,1},{6,2},{7,3},{8,12},{9,13},{10,... | collective-permute-start | bytes 196616 | tf_op jit(solution)/shard_map/ppermute | solution.py:491
  49.4 4.7 %collective-permute-start.6 = (f32[4,16,512]{2,1,0:T(8,128)S(1)}, f32[4,16,512]{2,1,0:T(8,128)S(1)}, u32[]{:S(2)}, u32[]{:S(2)}) collective-permute-start(f32[4,16,512]{2,1,0:T(8,128)S(1)} %pad_maximum_fusion.5), channel_id=1, source_target_pairs={{0,2},{1,3},{2,0},{3,1},{4,6},{5,7},{6,4},{7,5},{8,10},{9,11},{10,... | collective-permute-start | bytes 393224 | tf_op jit(solution)/shard_map/ppermute | solution.py:491
  54.2 2.5 %collective-permute-start.7 = (f32[8,16,512]{2,1,0:T(8,128)S(1)}, f32[8,16,512]{2,1,0:T(8,128)S(1)}, u32[]{:S(2)}, u32[]{:S(2)}) collective-permute-start(f32[8,16,512]{2,1,0:T(8,128)S(1)} %pad_maximum_fusion.2), channel_id=1, source_target_pairs={{0,1},{1,0},{2,3},{3,2},{4,5},{5,4},{6,7},{7,6},{8,9},{9,8},{10,11... | collective-permute-start | bytes 786440 | tf_op jit(solution)/shard_map/ppermute | solution.py:491
where the time goes:
time: 60.4 us; the launch traced here: 59.5 us
  Pallas kernels  22.6 us (37%)
  starting transfers between devices  20.8 us (34%)
  waiting for transfers between devices  12.7 us (21%)
  local copies, waits for them, and re-layouts  1.64 us (3%)
  between operations  1.57 us (3%)
    pallas_call x2, Pallas kernels, view_blocks(): pl.pallas_call(functools.partial(block_kernel, begin, so_far is not None)...  18.2 us
    ppermute x4, starting transfers between devices, gather_rounds(): other = lax.ppermute(held, 'row', [(i, i ^ step) for i in range(n_dev)])  11 us
    ppermute x4, starting transfers between devices, on_device(): other = lax.ppermute(message, 'row', [(i, i ^ step) for i in range(n_dev)])  9.74 us
    ppermute x4, waiting for transfers between devices, gather_rounds(): other = lax.ppermute(held, 'row', [(i, i ^ step) for i in range(n_dev)])  9.07 us
    ppermute x4, waiting for transfers between devices, on_device(): other = lax.ppermute(message, 'row', [(i, i ^ step) for i in range(n_dev)])  3.65 us
    pallas_call x1, Pallas kernels, second_bounce(): pl.pallas_call(bounce_kernel, out_shape=jax.ShapeDtypeStruct(emission.sha...  2.82 us
    unnamed x14, local copies, waits for them, and re-layouts  1.5 us
  transfers between devices with their start and end apart: 8, of which 6 were waited for; matrix products, arithmetic and copies ran while one was open for 0% of the time, Pallas kernels for 9%

commit v1 on v0

--- a/solution.py
+++ b/solution.py
@@ -245,11 +245,12 @@
 def block_kernel(
     begin, last, pay, words, left0, left1, left2, centres, refl, origin_ref, *refs
 ):
+    if begin:
+        so_far_hi, so_far_lo, *refs = refs
+    blocks, order, *refs = refs
     if last:
-        so_far_hi, so_far_lo, blocks, order, out_b, out_sums, out_scale, *refs = refs
-        acc_hi, acc_lo, *refs = refs
-    else:
-        blocks, order, acc_hi, acc_lo, *refs = refs
+        out_b, out_sums, out_scale, *refs = refs
+    acc_hi, acc_lo, *refs = refs
     (
         rhs1, rhs2, middle, next1, next2, next_middle, word_s, code_v, code, code_sem,
     ) = refs
@@ -280,8 +281,8 @@
     code_v[...] = table.astype(jnp.int32)
     to_scalar = pltpu.make_async_copy(code_v, code, code_sem)
     to_scalar.start()
-    acc_hi[...] = so_far_hi[...] if last else jnp.zeros_like(acc_hi)
-    acc_lo[...] = so_far_lo[...] if last else jnp.zeros_like(acc_lo)
+    acc_hi[...] = so_far_hi[...] if begin else jnp.zeros_like(acc_hi)
+    acc_lo[...] = so_far_lo[...] if begin else jnp.zeros_like(acc_lo)
     lane = lax.broadcasted_iota(jnp.int32, (1, TILE), 1)
     group_bit = jnp.left_shift(1, lane // (TILE // GROUPS))
     to_scalar.wait()
@@ -318,7 +319,8 @@
         ]
         source_factors(geo, origin, exact, next1, next2, next_middle)
 
-    def deposit(i):
+    def deposit(i, real):
+        i = jnp.maximum(i, 0)
         r, j, source = where_is(i)
         at = pl.multiple_of(2 * HOURS * source, HOURS)
         x = jnp.concatenate(
@@ -326,8 +328,10 @@
         )
         x_hi, x_lo = split2(x)
         ones = jnp.ones((16, TILE), BF16)
-        acc_hi[r] += mm_t(jnp.concatenate([x_hi, x_lo, ones], 0), blocks[i, 0])
-        acc_lo[r] += mm_t(jnp.concatenate([x_hi, ones], 0), blocks[i, 1])
+        hi = mm_t(jnp.concatenate([x_hi, x_lo, ones], 0), blocks[i, 0])
+        lo = mm_t(jnp.concatenate([x_hi, ones], 0), blocks[i, 1])
+        acc_hi[r] += jnp.where(real, hi, 0.0)
+        acc_lo[r] += jnp.where(real, lo, 0.0)
 
     def pair(exact, i, carry):
         r, j, _ = where_is(i)
@@ -339,6 +343,7 @@
             word_s[c * LANES : (c + 1) * LANES, :] = across(
                 words[j, pl.ds(2 * r + c, 1), :].astype(jnp.int32)
             )
+        deposit(i - 1, i > 0)
         prepare(i + 1, exact)
         for c in range(N_CH):
             rows = slice(c * CH, (c + 1) * CH)
@@ -369,7 +374,6 @@
             hi, lo = split2(total)
             blocks[i, 0, rows, :] = hi
             blocks[i, 1, rows, :] = lo
-        deposit(i)
         return carry
 
     for exact in (False, True):
@@ -379,6 +383,7 @@
             prepare(0, exact)
             lax.fori_loop(0, n, functools.partial(pair, exact), 0)
 
+    deposit(n - 1, n > 0)
     if not last:
         return
     for r in range(own):
@@ -392,7 +397,7 @@
         out_b[:, cols] = jnp.concatenate(emis, 1) + scale * irr
 
 
-def view_blocks(begin, pay, words, left, so_far=None):
+def view_blocks(begin, last, pay, words, left, so_far):
     vmem = pl.BlockSpec(memory_space=pltpu.VMEM)
     n_dev = pay.shape[0]
     width = left[4].shape[1]
@@ -407,15 +412,15 @@
         jax.ShapeDtypeStruct((2 * pairs,), jnp.int32),
     ]
     scratch = []
-    if so_far is None:
+    if not last:
         outs += sums
     else:
         outs += [jax.ShapeDtypeStruct((x, width), F32) for x in (HOURS, 1, 1)]
         scratch += [pltpu.VMEM(x.shape, F32) for x in sums]
-    args = [pay, words, *left, *(so_far or ())]
+    args = [pay, words, *left, *so_far]
     work = own * (n_dev - begin) // 2
     return pl.pallas_call(
-        functools.partial(block_kernel, begin, so_far is not None),
+        functools.partial(block_kernel, begin, last),
         out_shape=outs,
         in_specs=[vmem] * len(args),
         out_specs=[vmem, pl.BlockSpec(memory_space=pltpu.SMEM)] + [vmem] * (len(outs) - 2),
@@ -440,7 +445,8 @@
     )(*args)
 
 
-def bounce_kernel(order0, order1, field, blocks0, blocks1, scale, emis, out, acc):
+def bounce_kernel(field, scale, emis, *refs):
+    *lists, out, acc = refs
     own = out.shape[1] // TILE
     acc[...] = jnp.zeros_like(acc)
 
@@ -463,25 +469,25 @@
             acc[r] += jnp.where(live, got, 0.0)
         return carry
 
-    for order, blocks in ((order0, blocks0), (order1, blocks1)):
+    for blocks, order in zip(lists[0::2], lists[1::2]):
         lax.fori_loop(0, (order[0] + 3) // 4, functools.partial(some, order, blocks), 0)
     for r in range(own):
         cols = slice(r * TILE, (r + 1) * TILE)
         out[:, cols] = emis[:, cols] + scale[:, cols] * acc[r]
 
 
-def second_bounce(orders, field, blocks, scale, emission):
+def second_bounce(done, field, scale, emission):
     vmem = pl.BlockSpec(memory_space=pltpu.VMEM)
     own = emission.shape[1] // TILE
     return pl.pallas_call(
         bounce_kernel,
         out_shape=jax.ShapeDtypeStruct(emission.shape, F32),
-        in_specs=[pl.BlockSpec(memory_space=pltpu.SMEM)] * 2 + [vmem] * 5,
+        in_specs=[vmem] * 3 + [vmem, pl.BlockSpec(memory_space=pltpu.SMEM)] * len(done),
         out_specs=vmem,
         scratch_shapes=[pltpu.VMEM((own, HOURS, TILE), F32)],
         compiler_params=pltpu.CompilerParams(vmem_limit_bytes=12 << 20),
         name="second_bounce",
-    )(*orders, field, *blocks, scale, emission)
+    )(field, scale, emission, *sum(done, ()))
 
 
 def gather_rounds(x, n_dev):
@@ -499,29 +505,30 @@
     shared, words = pack(geometry, emission, occlusion, pair_recv, pair_src, pair_count)
     left = recv_factors(geometry, reflect[None])
     held, words = shared[None], words[None]
+    done, so_far, begin = [], [], 0
     step = n_dev // 2
     while step:
         lines = held.shape[0] * held.shape[1]
         keep, send = words[:, :step], words[:, step:]
         message = jnp.concatenate([held.reshape(-1, LANES), send.reshape(-1, LANES)], 0)
         other = lax.ppermute(message, "row", [(i, i ^ step) for i in range(n_dev)])
-        if step == n_dev // 4:
+        if step == n_dev // 2:
             other, left = lax.optimization_barrier((other, left))
-        if step == 2:
+        elif step == 2:
+            early = view_blocks(begin, False, held, words[:, 0], left, so_far)
+            other, early = lax.optimization_barrier((other, early))
+            done.append(tuple(early[:2]))
+            so_far = early[2:]
             begin = held.shape[0]
-            early = view_blocks(0, held, words[:, 0], left)
-            other, early = lax.optimization_barrier((other, early))
         held = jnp.concatenate([held, other[:lines].reshape(held.shape)], 0)
         words = jnp.concatenate([keep, other[lines:].reshape(send.shape)], 0)
         step //= 2
-    blocks0, order0, *so_far = early
-    blocks1, order1, field, sums, scale = view_blocks(
-        begin, held, words[:, 0], left, so_far
+    blocks, order, field, sums, scale = view_blocks(
+        begin, True, held, words[:, 0], left, so_far
     )
+    done.append((blocks, order))
     fields = gather_rounds(field, n_dev)
-    radiosity = second_bounce(
-        (order0, order1), fields, (blocks0, blocks1), scale, emission
-    )
+    radiosity = second_bounce(done, fields, scale, emission)
     return (radiosity, sums[0])
 
 

time: 60.4 us -> 59.4 us (0.983); the launches traced: 59.5 us -> 60.5 us
  starting transfers between devices: 20.8 us -> 11.8 us
  Pallas kernels: 22.6 us -> 29.1 us
  waiting for transfers between devices: 12.7 us -> 16.1 us
    ppermute x4, starting transfers between devices: 11 us -> 1.49 us  [gather_rounds(): other = lax.ppermute(held, 'row', [(i, i ^ step) for i in range(n_dev)])]
    pallas_call x2, Pallas kernels: 18.2 us -> 23.8 us  [view_blocks(): pl.pallas_call(functools.partial(block_kernel, begin, last), out_shape=ou...]
    ppermute x4, waiting for transfers between devices: 9.07 us -> 12.5 us  [gather_rounds(): other = lax.ppermute(held, 'row', [(i, i ^ step) for i in range(n_dev)])]
    pallas_call x1, Pallas kernels: 2.82 us -> 3.64 us  [second_bounce(): pl.pallas_call(bounce_kernel, out_shape=jax.ShapeDtypeStruct(emission.sha...]
  transfers between devices with their start and end apart: 8 -> 8, of which waited for: 6 -> 6; matrix products, arithmetic and copies ran while one was open for 0% -> 0% of each run, Pallas kernels for 9% -> 12%
where the time goes in v1:
time: 59.4 us; the launch traced here: 60.5 us
  Pallas kernels  29.1 us (49%)
  waiting for transfers between devices  16.1 us (27%)
  starting transfers between devices  11.8 us (20%)
  local copies, waits for them, and re-layouts  1.64 us (3%)
  between operations  1.58 us (3%)
    pallas_call x2, Pallas kernels, view_blocks(): pl.pallas_call(functools.partial(block_kernel, begin, last), out_shape=ou...  23.8 us
    ppermute x4, waiting for transfers between devices, gather_rounds(): other = lax.ppermute(held, 'row', [(i, i ^ step) for i in range(n_dev)])  12.5 us
    ppermute x4, starting transfers between devices, on_device(): other = lax.ppermute(message, 'row', [(i, i ^ step) for i in range(n_dev)])  10.3 us
    ppermute x4, waiting for transfers between devices, on_device(): other = lax.ppermute(message, 'row', [(i, i ^ step) for i in range(n_dev)])  3.65 us
    pallas_call x1, Pallas kernels, second_bounce(): pl.pallas_call(bounce_kernel, out_shape=jax.ShapeDtypeStruct(emission.sha...  3.64 us
    unnamed x14, local copies, waits for them, and re-layouts  1.5 us
    ppermute x4, starting transfers between devices, gather_rounds(): other = lax.ppermute(held, 'row', [(i, i ^ step) for i in range(n_dev)])  1.49 us
  transfers between devices with their start and end apart: 8, of which 6 were waited for; matrix products, arithmetic and copies ran while one was open for 0% of the time, Pallas kernels for 12%

profile of v1, /device:TPU:1, one launch (start us, length us, event | category | flops | bytes accessed | tf_op | source)
XLA Modules:
  0.0 60.5 jit_solution(6058154254659019104)
XLA Ops:
  1.3 1.0 %pack.1 = (f32[104,128]{1,0:T(8,128)S(1)}, f32[16,4,128]{2,1,0:T(4,128)S(1)}) custom-call(s32[1]{0:T(128)S(6)} %copy.29.count, s32[32]{0:T(128)} %recv_h.1, s32[32]{0:T(128)} %src_h.1, f32[9,512]{1,0:T(8,128)} %geo_ref.1, f32[16,512]{1,0:T(8,128)} %emis.1, s32[32,256]{1,0:T(8,128)} %occ_h.1), custom_call_target="tpu_custom_call" | custom-call | tf_op jit(solution)/shard_map/pack/pallas_call | solution.py:177
  2.3 3.2 %collective-permute-start = (f32[136,128]{1,0:T(8,128)S(1)}, f32[136,128]{1,0:T(8,128)S(1)}, u32[]{:S(2)}, u32[]{:S(2)}) collective-permute-start(f32[136,128]{1,0:T(8,128)S(1)} %pad_maximum_fusion.8), channel_id=1, source_target_pairs={{0,8},{1,9},{2,10},{3,11},{4,12},{5,13},{6,14},{7,15},{8,0},{9,1},... | collective-permute-start | bytes 208904 | tf_op jit(solution)/shard_map/ppermute | solution.py:514
  5.5 0.0 copy-start.1
  5.5 0.8 %copy-done.1 = f32[9,512]{1,0:T(8,128)S(1)} copy-done((f32[9,512]{1,0:T(8,128)S(1)}, f32[9,512]{1,0:T(8,128)}, u32[]{:S(2)}) %copy-start.1) | copy-done | bytes 18456
  6.3 0.0 copy-start.2
  6.3 0.7 %copy-done.2 = f32[512]{0:T(512)S(1)} copy-done((f32[512]{0:T(512)S(1)}, f32[512]{0:T(512)}, u32[]{:S(2)}) %copy-start.2) | copy-done | bytes 2072
  7.0 0.7 %recv_factors.1 = (bf16[16,128,48]{2,1,0:T(8,128)(2,1)S(1)}, bf16[16,128,48]{2,1,0:T(8,128)(2,1)S(1)}, bf16[512,48]{1,0:T(8,128)(2,1)S(1)}, f32[3,512,128]{2,1,0...) custom-call(f32[9,512]{1,0:T(8,128)S(1)} %copy-done.1, f32[1,512]{1,0:T(1,128)S(1)} %bitcast.38), custom_call_target="tpu_custom_call" | custom-call | flops 200000 | bytes 1600000 | tf_op jit(solution)/shard_map/recv_factors/pallas_call | solution.py:109
  7.6 0.0 collective-permute-done
  7.7 2.0 %collective-permute-start.1 = (f32[240,128]{1,0:T(8,128)S(1)}, f32[240,128]{1,0:T(8,128)S(1)}, u32[]{:S(2)}, u32[]{:S(2)}) collective-permute-start(f32[240,128]{1,0:T(8,128)S(1)} %pad_maximum_fusion.6), channel_id=1, source_target_pairs={{0,4},{1,5},{2,6},{3,7},{4,0},{5,1},{6,2},{7,3},{8,12},{9,13},{10,... | collective-permute-start | bytes 368648 | tf_op jit(solution)/shard_map/ppermute | solution.py:514
  9.8 2.3 %collective-permute-done.1 = f32[240,128]{1,0:T(8,128)S(1)} collective-permute-done((f32[240,128]{1,0:T(8,128)S(1)}, f32[240,128]{1,0:T(8,128)S(1)}, u32[]{:S(2)}, u32[]{:S(2)}) %collective-permute-start.1) | collective-permute-done | bytes 122912 | tf_op jit(solution)/shard_map/ppermute | solution.py:514
  12.2 1.3 %collective-permute-start.2 = (f32[448,128]{1,0:T(8,128)S(1)}, f32[448,128]{1,0:T(8,128)S(1)}, u32[]{:S(2)}, u32[]{:S(2)}) collective-permute-start(f32[448,128]{1,0:T(8,128)S(1)} %pad_maximum_fusion.3), channel_id=1, source_target_pairs={{0,2},{1,3},{2,0},{3,1},{4,6},{5,7},{6,4},{7,5},{8,10},{9,11},{10,... | collective-permute-start | bytes 688136 | tf_op jit(solution)/shard_map/ppermute | solution.py:514
  13.5 6.8 %view_blocks.2 = (bf16[8,2,256,256]{3,2,1,0:T(8,128)(2,1)S(1)}, s32[16]{0:T(128)S(1)}, f32[2,48,256]{2,1,0:T(8,128)S(1)}, f32[2,32,256]{2,1,0:T(8,128)S(1)}) custom-call(f32[4,104,128]{2,1,0:T(8,128)S(1)} %pad_maximum_fusion.4.pay, f32[4,4,128]{2,1,0:T(4,128)S(1)} %maximum_bitcast_fusion.words, bf16[16,128,48]{2,1,0:T(8,128)(2,1)S(1)} %get-tuple-element.40.left0, ...), custom_call_target="tpu_custom_call" | custom-call | flops 4000000000 | bytes 1048576 | tf_op jit(solution)/shard_map/view_blocks/pallas_call | solution.py:422
  20.3 0.0 collective-permute-done.2
  20.4 3.8 %collective-permute-start.3 = (f32[864,128]{1,0:T(8,128)S(1)}, f32[864,128]{1,0:T(8,128)S(1)}, u32[]{:S(2)}, u32[]{:S(2)}) collective-permute-start(f32[864,128]{1,0:T(8,128)S(1)} %pad_maximum_fusion), channel_id=1, source_target_pairs={{0,1},{1,0},{2,3},{3,2},{4,5},{5,4},{6,7},{7,6},{8,9},{9,8},{10,11... | collective-permute-start | bytes 1327112 | tf_op jit(solution)/shard_map/ppermute | solution.py:514
  24.2 1.4 %collective-permute-done.3 = f32[864,128]{1,0:T(8,128)S(1)} collective-permute-done((f32[864,128]{1,0:T(8,128)S(1)}, f32[864,128]{1,0:T(8,128)S(1)}, u32[]{:S(2)}, u32[]{:S(2)}) %collective-permute-start.3) | collective-permute-done | bytes 442400 | tf_op jit(solution)/shard_map/ppermute | solution.py:514
  25.7 0.0 copy-start
  25.7 17.0 %view_blocks.3 = (bf16[24,2,256,256]{3,2,1,0:T(8,128)(2,1)S(1)}, s32[64]{0:T(128)S(1)}, f32[16,512]{1,0:T(8,128)S(1)}, f32[1,512]{1,0:T(1,128)}, f32[1,512]{1,0:T(1,128)S(1)}) custom-call(f32[16,104,128]{2,1,0:T(8,128)S(1)} %constant_dynamic-update-slice_fusion.pay, f32[16,4,128]{2,1,0:T(4,128)S(1)} %fusion.1.words, ...), custom_call_target="tpu_custom_call" | custom-call | flops 12000000000 | bytes 3145728 | tf_op jit(solution)/shard_map/view_blocks/pallas_call | solution.py:422
  42.7 0.1 collective-permute-start.4
  42.8 3.7 %collective-permute-done.4 = f32[1,16,512]{2,1,0:T(8,128)S(1)} collective-permute-done((f32[1,16,512]{2,1,0:T(8,128)S(1)}, f32[1,16,512]{2,1,0:T(8,128)S(1)}, u32[]{:S(2)}, u32[]{:S(2)}) %collective-permute-start.4) | collective-permute-done | bytes 32800 | tf_op jit(solution)/shard_map/ppermute | solution.py:497
  46.5 0.0 collective-permute-start.5
  46.5 3.1 %collective-permute-done.5 = f32[2,16,512]{2,1,0:T(8,128)S(1)} collective-permute-done((f32[2,16,512]{2,1,0:T(8,128)S(1)}, f32[2,16,512]{2,1,0:T(8,128)S(1)}, u32[]{:S(2)}, u32[]{:S(2)}) %collective-permute-start.5) | collective-permute-done | bytes 65568 | tf_op jit(solution)/shard_map/ppermute | solution.py:497
  49.6 0.1 collective-permute-start.6
  49.7 4.6 %collective-permute-done.6 = f32[4,16,512]{2,1,0:T(8,128)S(1)} collective-permute-done((f32[4,16,512]{2,1,0:T(8,128)S(1)}, f32[4,16,512]{2,1,0:T(8,128)S(1)}, u32[]{:S(2)}, u32[]{:S(2)}) %collective-permute-start.6) | collective-permute-done | bytes 131104 | tf_op jit(solution)/shard_map/ppermute | solution.py:497
  54.3 1.3 %collective-permute-start.7 = (f32[8,16,512]{2,1,0:T(8,128)S(1)}, f32[8,16,512]{2,1,0:T(8,128)S(1)}, u32[]{:S(2)}, u32[]{:S(2)}) collective-permute-start(f32[8,16,512]{2,1,0:T(8,128)S(1)} %pad_maximum_fusion.2), channel_id=1, source_target_pairs={{0,1},{1,0},{2,3},{3,2},{4,5},{5,4},{6,7},{7,6},{8,9},{9,8},{10,11... | collective-permute-start | bytes 786440 | tf_op jit(solution)/shard_map/ppermute | solution.py:497
  55.7 1.1 %collective-permute-done.7 = f32[8,16,512]{2,1,0:T(8,128)S(1)} collective-permute-done((f32[8,16,512]{2,1,0:T(8,128)S(1)}, f32[8,16,512]{2,1,0:T(8,128)S(1)}, u32[]{:S(2)}, u32[]{:S(2)}) %collective-permute-start.7) | collective-permute-done | bytes 262176 | tf_op jit(solution)/shard_map/ppermute | solution.py:497
  56.8 0.0 copy-done
  56.8 3.6 %second_bounce.1 = f32[16,512]{1,0:T(8,128)} custom-call(f32[16,16,512]{2,1,0:T(8,128)S(1)} %constant_dynamic-update-slice_fusion.5.field, f32[1,512]{1,0:T(1,128)S(1)} %get-tuple-element.54.scale, f32[16,512]{1,0:T(8,128)S(1)} %copy-done, bf16[8,2,256,256]{3,2,1,0:T(8,128)(2,1)S(1)} %get-tuple-element.55.refs_0_, s32[16]{0:T(128)S(1)} %get-tuple-element.56.refs_1_, ...), custom_call_target="tpu_custom_call" | custom-call | tf_op jit(solution)/shard_map/second_bounce/pallas_call | solution.py:482
  (37 shorter events, 0.4 us)
Async XLA Ops:
  2.3 5.3 %collective-permute-start = (f32[136,128]{1,0:T(8,128)S(1)}, f32[136,128]{1,0:T(8,128)S(1)}, u32[]{:S(2)}, u32[]{:S(2)}) collective-permute-start(f32[136,128]{1,0:T(8,128)S(1)} %pad_maximum_fusion.8), channel_id=1, source_target_pairs={{0,8},{1,9},{2,10},{3,11},{4,12},{5,13},{6,14},{7,15},{8,0},{9,1},... | collective-permute-start | bytes 208904 | tf_op jit(solution)/shard_map/ppermute | solution.py:514
  5.5 0.8 %copy-start.1 = (f32[9,512]{1,0:T(8,128)S(1)}, f32[9,512]{1,0:T(8,128)}, u32[]{:S(2)}) copy-start(f32[9,512]{1,0:T(8,128)} %geo_ref.1) | copy-start | bytes 55300
  6.3 0.7 %copy-start.2 = (f32[512]{0:T(512)S(1)}, f32[512]{0:T(512)}, u32[]{:S(2)}) copy-start(f32[512]{0:T(512)} %param.9) | copy-start | bytes 6148
  7.7 4.3 %collective-permute-start.1 = (f32[240,128]{1,0:T(8,128)S(1)}, f32[240,128]{1,0:T(8,128)S(1)}, u32[]{:S(2)}, u32[]{:S(2)}) collective-permute-start(f32[240,128]{1,0:T(8,128)S(1)} %pad_maximum_fusion.6), channel_id=1, source_target_pairs={{0,4},{1,5},{2,6},{3,7},{4,0},{5,1},{6,2},{7,3},{8,12},{9,13},{10,... | collective-permute-start | bytes 368648 | tf_op jit(solution)/shard_map/ppermute | solution.py:514
  12.2 8.1 %collective-permute-start.2 = (f32[448,128]{1,0:T(8,128)S(1)}, f32[448,128]{1,0:T(8,128)S(1)}, u32[]{:S(2)}, u32[]{:S(2)}) collective-permute-start(f32[448,128]{1,0:T(8,128)S(1)} %pad_maximum_fusion.3), channel_id=1, source_target_pairs={{0,2},{1,3},{2,0},{3,1},{4,6},{5,7},{6,4},{7,5},{8,10},{9,11},{10,... | collective-permute-start | bytes 688136 | tf_op jit(solution)/shard_map/ppermute | solution.py:514
  20.4 5.2 %collective-permute-start.3 = (f32[864,128]{1,0:T(8,128)S(1)}, f32[864,128]{1,0:T(8,128)S(1)}, u32[]{:S(2)}, u32[]{:S(2)}) collective-permute-start(f32[864,128]{1,0:T(8,128)S(1)} %pad_maximum_fusion), channel_id=1, source_target_pairs={{0,1},{1,0},{2,3},{3,2},{4,5},{5,4},{6,7},{7,6},{8,9},{9,8},{10,11... | collective-permute-start | bytes 1327112 | tf_op jit(solution)/shard_map/ppermute | solution.py:514
  25.7 31.1 %copy-start = (f32[16,512]{1,0:T(8,128)S(1)}, f32[16,512]{1,0:T(8,128)}, u32[]{:S(2)}) copy-start(f32[16,512]{1,0:T(8,128)} %emis.1) | copy-start | bytes 98308
  42.7 3.7 %collective-permute-start.4 = (f32[1,16,512]{2,1,0:T(8,128)S(1)}, f32[1,16,512]{2,1,0:T(8,128)S(1)}, u32[]{:S(2)}, u32[]{:S(2)}) collective-permute-start(f32[1,16,512]{2,1,0:T(8,128)S(1)} %bitcast.33), channel_id=1, source_target_pairs={{0,8},{1,9},{2,10},{3,11},{4,12},{5,13},{6,14},{7,15},{8,0},{9,1},... | collective-permute-start | bytes 98312 | tf_op jit(solution)/shard_map/ppermute | solution.py:497
  46.5 3.1 %collective-permute-start.5 = (f32[2,16,512]{2,1,0:T(8,128)S(1)}, f32[2,16,512]{2,1,0:T(8,128)S(1)}, u32[]{:S(2)}, u32[]{:S(2)}) collective-permute-start(f32[2,16,512]{2,1,0:T(8,128)S(1)} %pad_maximum_fusion.9), channel_id=1, source_target_pairs={{0,4},{1,5},{2,6},{3,7},{4,0},{5,1},{6,2},{7,3},{8,12},{9,13},{10,... | collective-permute-start | bytes 196616 | tf_op jit(solution)/shard_map/ppermute | solution.py:497
  49.6 4.7 %collective-permute-start.6 = (f32[4,16,512]{2,1,0:T(8,128)S(1)}, f32[4,16,512]{2,1,0:T(8,128)S(1)}, u32[]{:S(2)}, u32[]{:S(2)}) collective-permute-start(f32[4,16,512]{2,1,0:T(8,128)S(1)} %pad_maximum_fusion.5), channel_id=1, source_target_pairs={{0,2},{1,3},{2,0},{3,1},{4,6},{5,7},{6,4},{7,5},{8,10},{9,11},{10,... | collective-permute-start | bytes 393224 | tf_op jit(solution)/shard_map/ppermute | solution.py:497
  54.3 2.5 %collective-permute-start.7 = (f32[8,16,512]{2,1,0:T(8,128)S(1)}, f32[8,16,512]{2,1,0:T(8,128)S(1)}, u32[]{:S(2)}, u32[]{:S(2)}) collective-permute-start(f32[8,16,512]{2,1,0:T(8,128)S(1)} %pad_maximum_fusion.2), channel_id=1, source_target_pairs={{0,1},{1,0},{2,3},{3,2},{4,5},{5,4},{6,7},{7,6},{8,9},{9,8},{10,11... | collective-permute-start | bytes 786440 | tf_op jit(solution)/shard_map/ppermute | solution.py:497
